TPU v7x, 32 devices: a whole 2x2x4 slice. The times are simulated.
32 devices in a mesh: dp: 8 (over z, y), expert: 4 (over x, core).
Axes of the slice: x: 2, y: 2, z: 4, core: 2. Of those that a mesh axis runs over, the one named last changes fastest.
Arguments:
- tokens: bfloat16 [1024, 4096], P('dp'), may hold values from -6 to 6
- upstream: bfloat16 [1024, 4096], P('dp', 'expert'), may hold values from -6 to 6
- gates: bfloat16 [1024, 2], P('dp'), may hold values from 0.049804688 to 1
- expert_ids: int32 [1024, 2], P('dp'), may hold values from 0 to 7, all different within a row; in each aligned block of 128 rows (0 to 127, 128 to 255, ...) at most 64 rows name the same one
- w_gate: bfloat16 [8, 1536, 4096], P('dp', 'expert'), may hold values from -0.09375 to 0.09375
- w_up: bfloat16 [8, 1536, 4096], P('dp', 'expert'), may hold values from -0.09375 to 0.09375
- w_down: bfloat16 [8, 1536, 4096], P('dp', 'expert'), may hold values from -0.15625 to 0.15625
Outputs:
- grad_x: bfloat16 [1024, 4096], P('dp', 'expert')
- grad_gates: float32 [1024, 2], P('dp')
- grad_w_gate: bfloat16 [8, 1536, 4096], P('dp', 'expert')
- grad_w_up: bfloat16 [8, 1536, 4096], P('dp', 'expert')
- grad_w_down: bfloat16 [8, 1536, 4096], P('dp', 'expert')
Inputs may be any that keep to these rules, and one draw needn't show every extreme that they name: `expert_ids`: each row names 2 different experts. In each aligned block of 128 rows (the tokens of one index of dp) no expert is named by more than 64 rows, a bound that some block reaches.
All inputs are finite; a program needn't handle non-finite values.
Results may differ from a plain program's by a relative error of at most 0.012.
Values may be sent and summed in bfloat16 or wider, within the bound.
A program may use at most 128 MiB of HBM per device.

v0:
```python
import jax
import jax.numpy as jnp
from jax import lax
from jax.sharding import PartitionSpec as P


def swish_pair(pre):
    sigma = jax.nn.sigmoid(pre)
    return (pre * sigma, sigma * (1.0 + pre * (1.0 - sigma)))


def contract_last(left, right):
    return lax.dot_general(
        left, right, (((1,), (1,)), ((), ())), preferred_element_type=jnp.float32
    )


def contract_first(left, right):
    return lax.dot_general(
        left, right, (((0,), (0,)), ((), ())), preferred_element_type=jnp.float32
    )


def expert_backward(inputs, upward, scale_col, w_g, w_u, w_d):
    pre_gate = contract_last(inputs, w_g)
    pre_up = contract_last(inputs, w_u)
    swish, slope = swish_pair(pre_gate)
    act = (swish * pre_up).astype(jnp.bfloat16)
    act_f = act.astype(jnp.float32)
    back = contract_last(upward, w_d)
    gate_term = jnp.sum(act_f * back, axis=1)
    scaled = (scale_col * act_f).astype(jnp.bfloat16)
    grad_down = contract_first(scaled, upward).astype(jnp.bfloat16)
    weighted = scale_col * back
    d_gate = (weighted * pre_up * slope).astype(jnp.bfloat16)
    d_up = (weighted * swish).astype(jnp.bfloat16)
    grad_gate = contract_first(d_gate, inputs).astype(jnp.bfloat16)
    grad_up = contract_first(d_up, inputs).astype(jnp.bfloat16)
    piece = jnp.dot(d_gate, w_g, preferred_element_type=jnp.float32)
    piece = piece + jnp.dot(d_up, w_u, preferred_element_type=jnp.float32)
    return (piece.astype(jnp.bfloat16), gate_term, grad_gate, grad_up, grad_down)


def per_device(tokens, upstream, gates, expert_ids, w_gate, w_up, w_down):
    groups = lax.axis_size("dp")
    experts = groups * w_gate.shape[0]
    tok_rows, width = tokens.shape
    top = expert_ids.shape[1]
    cap = 2 * tok_rows * top // experts
    part = upstream.shape[1]
    rows = experts * cap
    own = lax.axis_index("expert")
    tok_part = lax.dynamic_slice_in_dim(tokens, own * part, part, axis=1)
    flat = expert_ids.reshape(-1)
    count = flat.shape[0]
    earlier = jnp.arange(count)[None, :] < jnp.arange(count)[:, None]
    same = flat[:, None] == flat[None, :]
    position = jnp.sum((earlier & same).astype(jnp.int32), axis=1)
    slot = (flat * cap + position).reshape(tok_rows, top)
    hit = slot[None, :, :] == jnp.arange(rows, dtype=jnp.int32)[:, None, None]
    pick = jnp.sum(hit.astype(jnp.float32), axis=2).astype(jnp.bfloat16)
    scale = jnp.sum(jnp.where(hit, gates.astype(jnp.float32)[None], 0.0), axis=(1, 2))
    packed = jnp.concatenate([tok_part, upstream], axis=1)
    send = jnp.dot(pick, packed, preferred_element_type=jnp.float32).astype(jnp.bfloat16)
    send = jnp.concatenate(
        [send, jnp.broadcast_to(scale[:, None], (rows, 128)).astype(jnp.bfloat16)], axis=1
    )
    got = lax.all_to_all(send, "dp", split_axis=0, concat_axis=0, tiled=True)
    inputs = lax.all_gather(got[:, :part], "expert", axis=1, tiled=True)
    upward = lax.all_gather(got[:, part : 2 * part], "expert", axis=1, tiled=True)
    scale_col = got[:, 2 * part : 2 * part + 1].astype(jnp.float32)
    piece, term, grad_gate, grad_up, grad_down = expert_backward(
        inputs, upward, scale_col, w_gate[0], w_up[0], w_down[0]
    )
    total = lax.psum(term, "expert")
    summed = lax.psum_scatter(piece, "expert", scatter_dimension=1, tiled=True)
    high = total.astype(jnp.bfloat16)
    low = (total - high.astype(jnp.float32)).astype(jnp.bfloat16)
    lane = lax.broadcasted_iota(jnp.int32, (rows, 128), 1)
    tail = jnp.where(lane == 0, high[:, None], low[:, None])
    home = lax.all_to_all(
        jnp.concatenate([summed, tail], axis=1), "dp", split_axis=0, concat_axis=0, tiled=True
    )
    grad_x = contract_first(pick, home[:, :part]).astype(jnp.bfloat16)
    terms = home[:, part].astype(jnp.float32) + home[:, part + 1].astype(jnp.float32)
    grad_gates = jnp.sum(jnp.where(hit, terms[:, None, None], 0.0), axis=0)
    return (grad_x, grad_gates, grad_gate[None], grad_up[None], grad_down[None])


def solution(mesh):
    in_specs = (
        P("dp", None),
        P("dp", "expert"),
        P("dp", None),
        P("dp", None),
        P("dp", "expert", None),
        P("dp", "expert", None),
        P("dp", "expert", None),
    )
    out_specs = (
        P("dp", "expert"),
        P("dp", None),
        P("dp", "expert", None),
        P("dp", "expert", None),
        P("dp", "expert", None),
    )
    return jax.shard_map(
        per_device, mesh=mesh, in_specs=in_specs, out_specs=out_specs, check_vma=False
    )
```

profile of v0, /device:TPU:0, one launch (start us, length us, event | category | flops | bytes accessed | tf_op | source)
XLA Modules:
  0.0 249.7 jit_solution(17244349848035692851)
XLA Ops:
  7.2 0.9 copy.28
  8.3 0.2 convert_reduce_fusion.2
  8.7 0.7 multiply_add_fusion
  9.4 0.7 convert_element_type.79
  10.1 1.0 constant_dynamic-slice_fusion
  11.0 0.2 convert_reduce_fusion
  11.2 1.6 convolution_convert_fusion.3
  13.0 0.2 pad_maximum_fusion
  13.2 58.5 %all_to_all.24 = bf16[8,64,2176]{2,1,0:T(8,128)(2,1)S(1)} all-to-all(bf16[8,64,2176]{2,1,0:T(8,128)(2,1)S(1)} %bitcast.39), channel_id=1, replica_groups=mesh['dp'=8,'expert'=4] {'dp'}, dimensions={0} | all-to-all | bytes 4456448 | tf_op jit(solution)/shard_map/all_to_all | solution.py:68
  71.7 1.4 copy-done.1
  73.0 1.6 fusion.25
  74.7 0.7 all-gather.3.cloned.1.call-update
  75.5 1.0 convert_reduce_fusion.1
  76.5 31.5 %all-gather.5.cloned.1.call-done = bf16[512,4096]{1,0:T(8,128)(2,1)} async-done(((bf16[512,1024]{1,0:T(8,128)(2,1)}), bf16[512,4096]{1,0:T(8,128)(2,1)}) %all-gather.5.cloned.1.call-update) | async-done | bytes 4194320 | tf_op jit(solution)/shard_map/all_gather | solution.py:69
  108.0 5.0 %fusion.5 = f32[512,384]{0,1:T(8,128)} fusion(bf16[512,4096]{1,0:T(8,128)(2,1)} %all-gather.5.cloned.1.call-done, bf16[1,384,4096]{2,1,0:T(8,128)(2,1)S(1)} %copy-done), kind=kOutput, calls=%fused_computation.9 | convolution fusion | flops 1610612736 | bytes 8126464 | tf_op jit(solution)/shard_map/dot_general | solution.py:13
  113.0 2.7 %fusion.8 = f32[512,384]{0,1:T(8,128)} fusion(bf16[512,4096]{1,0:T(8,128)(2,1)S(1)} %copy-done.7, bf16[1,384,4096]{2,1,0:T(8,128)(2,1)S(1)} %copy-done.2), kind=kOutput, calls=%fused_computation.12 | convolution fusion | flops 1610612736 | bytes 8126464 | tf_op jit(solution)/shard_map/dot_general | solution.py:13
  115.7 28.9 %all-gather.3.cloned.1.call-done = bf16[512,4096]{1,0:T(8,128)(2,1)} async-done(((bf16[512,1024]{1,0:T(8,128)(2,1)}), bf16[512,4096]{1,0:T(8,128)(2,1)}) %all-gather.3.cloned.1.call-update) | async-done | bytes 4194320 | tf_op jit(solution)/shard_map/all_gather | solution.py:70
  144.6 6.4 %fusion.13 = (f32[512]{0:T(512)S(1)}, bf16[512,384]{0,1:T(8,128)(2,1)}, bf16[512,384]{0,1:T(8,128)(2,1)S(1)}, bf16[512,384]{0,1:T(8,128)(2,1)S(1)}) fusion(f32[512,384]{0,1:T(8,128)} %fusion.8, f32[512,384]{0,1:T(8,128)} %fusion.5, f32[512]{0:T(512)S(1)} %convert_reduce_fusion.1, bf16[512,4096]{1,0:T(8,128)(2,1)} %all-gather.3.cloned.1.call-done, ...), kind=kOutput, calls=%fused_computation.23 | convolution fusion | flops 1614347776 | bytes 10096640 | tf_op jit(solution)/shard_map/dot_general | solution.py:13
  151.0 2.4 fusion.3
  153.4 4.6 %add_convert_fusion = bf16[512,4096]{1,0:T(8,128)(2,1)} fusion(f32[512,4096]{1,0:T(8,128)S(1)} %fusion.3, bf16[512,384]{0,1:T(8,128)(2,1)S(1)} %get-tuple-element.14, bf16[1,384,4096]{2,1,0:T(8,128)(2,1)S(1)} %copy-done.3), kind=kOutput, calls=%fused_computation | convolution fusion | flops 1614807040 | bytes 16121856 | tf_op jit(solution)/shard_map/dot_general | solution.py:40
  158.0 5.9 %psum.7 = f32[512]{0:T(512)S(1)} all-reduce(f32[512]{0:T(512)S(1)} %get-tuple-element.9), channel_id=1, replica_groups=mesh['dp'=8,'expert'=4] {'expert'}, use_global_device_ids=true, to_apply=%region_5.6 | all-reduce | flops 512 | bytes 4096 | tf_op jit(solution)/shard_map/psum | solution.py:75
  163.9 0.2 broadcast_select_fusion
  164.1 38.5 %reduce-scatter.2.cloned.1.call-done = bf16[512,1024]{1,0:T(8,128)(2,1)} async-done(((bf16[512,4096]{1,0:T(8,128)(2,1)}), bf16[512,1024]{1,0:T(8,128)(2,1)}) %reduce-scatter.2.cloned.1.call-update) | async-done | bytes 1048592 | tf_op jit(solution)/shard_map/reduce_scatter | solution.py:76
  202.6 2.4 pad_maximum_fusion.1
  205.0 5.5 %all-to-all-start.1 = ((bf16[8,64,1152]{2,1,0:T(8,128)(2,1)}), bf16[8,64,1152]{2,1,0:T(8,128)(2,1)}, u32[]{:S(2)}, u32[]{:S(2)}) async-start(bf16[8,64,1152]{2,1,0:T(8,128)(2,1)} %bitcast.40), calls=%async_computation.2 | async-start | bytes 2359296 | tf_op jit(solution)/shard_map/all_to_all | solution.py:81
  210.5 5.9 %fusion = bf16[1,384,4096]{2,1,0:T(8,128)(2,1)} fusion(bf16[512,384]{0,1:T(8,128)(2,1)} %copy-done.6, bf16[512,4096]{1,0:T(8,128)(2,1)} %all-gather.5.cloned.1.call-done), kind=kOutput, calls=%fused_computation.4 | convolution fusion | flops 1612185600 | bytes 7733248 | tf_op jit(solution)/shard_map/dot_general | solution.py:19
  216.5 3.5 %fusion.1 = bf16[1,384,4096]{2,1,0:T(8,128)(2,1)} fusion(bf16[512,384]{0,1:T(8,128)(2,1)S(1)} %copy-done.5, bf16[512,4096]{1,0:T(8,128)(2,1)S(1)} %copy-done.8), kind=kOutput, calls=%fused_computation.5 | convolution fusion | flops 1612185600 | bytes 7733248 | tf_op jit(solution)/shard_map/dot_general | solution.py:19
  219.9 3.5 %fusion.2 = bf16[1,384,4096]{2,1,0:T(8,128)(2,1)} fusion(bf16[512,4096]{1,0:T(8,128)(2,1)S(1)} %copy-done.9, bf16[512,384]{0,1:T(8,128)(2,1)S(1)} %copy-done.10, f32[512]{0:T(512)S(1)} %convert_reduce_fusion.1), kind=kOutput, calls=%fused_computation.6 | convolution fusion | flops 1612775424 | bytes 7735296 | tf_op jit(solution)/shard_map/dot_general | solution.py:19
  223.4 15.6 %all-to-all-done.1 = bf16[8,64,1152]{2,1,0:T(8,128)(2,1)} async-done(((bf16[8,64,1152]{2,1,0:T(8,128)(2,1)}), bf16[8,64,1152]{2,1,0:T(8,128)(2,1)}, u32[]{:S(2)}, u32[]{:S(2)}) %all-to-all-start.1) | async-done | bytes 1179680 | tf_op jit(solution)/shard_map/all_to_all | solution.py:81
  239.0 2.3 convolution_convert_fusion.4
  241.3 1.2 add_reduce_fusion
  242.5 0.7 select_reduce_fusion
  (32 shorter events, 0.7 us)
Async XLA Ops:
  7.2 100.8 %copy-start = (bf16[1,384,4096]{2,1,0:T(8,128)(2,1)S(1)}, bf16[1,384,4096]{2,1,0:T(8,128)(2,1)}, u32[]{:S(2)}) copy-start(bf16[1,384,4096]{2,1,0:T(8,128)(2,1)} %param.11) | copy-start | bytes 9437188
  7.2 100.8 %all-gather.5.cloned.1.call-start = ((), (), s32[]{:S(2)}) async-start(), calls=%async_computation.4 | async-start | bytes 5242880 | tf_op jit(solution)/shard_map/all_gather | solution.py:69
  71.7 1.4 copy-start.1
  74.7 69.9 %all-gather.3.cloned.1.call-start = ((), (), s32[]{:S(2)}) async-start(), calls=%async_computation.3 | async-start | bytes 5242880 | tf_op jit(solution)/shard_map/all_gather | solution.py:70
  75.4 127.2 %reduce-scatter.2.cloned.1.call-start = ((), (), s32[]{:S(2)}) async-start(), calls=%async_computation.5 | async-start | bytes 5242880 | tf_op jit(solution)/shard_map/reduce_scatter | solution.py:76
  108.0 5.0 %copy-start.2 = (bf16[1,384,4096]{2,1,0:T(8,128)(2,1)S(1)}, bf16[1,384,4096]{2,1,0:T(8,128)(2,1)}, u32[]{:S(2)}) copy-start(bf16[1,384,4096]{2,1,0:T(8,128)(2,1)} %param.12) | copy-start | bytes 9437188
  108.0 5.0 %copy-start.7 = (bf16[512,4096]{1,0:T(8,128)(2,1)S(1)}, bf16[512,4096]{1,0:T(8,128)(2,1)}, u32[]{:S(2)}) copy-start(bf16[512,4096]{1,0:T(8,128)(2,1)} %all-gather.5.cloned.1.call-done) | copy-start | bytes 12582916
  151.0 2.4 copy-start.6
  151.0 2.4 copy-start.4
  151.0 2.4 copy-start.3
  205.0 34.0 %all-to-all-start.1 = ((bf16[8,64,1152]{2,1,0:T(8,128)(2,1)}), bf16[8,64,1152]{2,1,0:T(8,128)(2,1)}, u32[]{:S(2)}, u32[]{:S(2)}) async-start(bf16[8,64,1152]{2,1,0:T(8,128)(2,1)} %bitcast.40), calls=%async_computation.2 | async-start | bytes 2359296 | tf_op jit(solution)/shard_map/all_to_all | solution.py:81
  210.5 5.9 %copy-start.5 = (bf16[512,384]{0,1:T(8,128)(2,1)S(1)}, bf16[512,384]{0,1:T(8,128)(2,1)}, u32[]{:S(2)}) copy-start(bf16[512,384]{0,1:T(8,128)(2,1)} %copy-done.4) | copy-start | bytes 1179652
  210.5 5.9 %copy-start.8 = (bf16[512,4096]{1,0:T(8,128)(2,1)S(1)}, bf16[512,4096]{1,0:T(8,128)(2,1)}, u32[]{:S(2)}) copy-start(bf16[512,4096]{1,0:T(8,128)(2,1)} %all-gather.5.cloned.1.call-done) | copy-start | bytes 12582916
  216.4 3.5 %copy-start.9 = (bf16[512,4096]{1,0:T(8,128)(2,1)S(1)}, bf16[512,4096]{1,0:T(8,128)(2,1)}, u32[]{:S(2)}) copy-start(bf16[512,4096]{1,0:T(8,128)(2,1)} %all-gather.3.cloned.1.call-done) | copy-start | bytes 12582916
  216.4 3.5 %copy-start.10 = (bf16[512,384]{0,1:T(8,128)(2,1)S(1)}, bf16[512,384]{0,1:T(8,128)(2,1)}, u32[]{:S(2)}) copy-start(bf16[512,384]{0,1:T(8,128)(2,1)} %get-tuple-element.10) | copy-start | bytes 1179652
Sparse Core Ops, SparseCore 0:
  74.8 33.1 all-gather.4
  110.1 34.4 all-gather.2
  158.1 44.4 reduce-scatter.1
where the time goes:
time: 250 us
  waiting for transfers between devices  115 us (46%)
  blocking collectives  64.4 us (26%)
  matrix products  37.9 us (15%)
  between operations  13.9 us (6%)
  other arithmetic  7.47 us (3%)
  starting transfers between devices  5.61 us (2%)
  local copies, waits for them, and re-layouts  5.38 us (2%)
    all_to_all x1, blocking collectives, per_device(): got = lax.all_to_all(send, 'dp', split_axis=0, concat_axis=0, tiled=True)  58.5 us
    reduce_scatter x1, waiting for transfers between devices, per_device(): summed = lax.psum_scatter(piece, 'expert', scatter_dimension=1, tiled=True)  38.5 us
    all_gather x1, waiting for transfers between devices, per_device(): inputs = lax.all_gather(got[:, :part], 'expert', axis=1, tiled=True)  31.5 us
    all_gather x1, waiting for transfers between devices, per_device(): upward = lax.all_gather(got[:, part:2 * part], 'expert', axis=1, tiled=True)  28.9 us
    all_to_all x1, waiting for transfers between devices, per_device(): lax.all_to_all(jnp.concatenate([summed, tail], axis=1), 'dp', split_axis=...  15.6 us
    dot_general x4, matrix products, contract_first(): lax.dot_general(left, right, (((0,), (0,)), ((), ())), preferred_element_...  15.1 us
    dot_general x3, matrix products, contract_last(): lax.dot_general(left, right, (((1,), (1,)), ((), ())), preferred_element_...  14.1 us
    psum x1, blocking collectives, per_device(): total = lax.psum(term, 'expert')  5.9 us
  transfers between devices with their start and end apart: 4, of which 4 were waited for; matrix products, arithmetic and copies ran while one was open for 9% of the time, Pallas kernels for 0%

commit v1 on v0

--- a/solution.py
+++ b/solution.py
@@ -67,7 +67,7 @@
     )
     got = lax.all_to_all(send, "dp", split_axis=0, concat_axis=0, tiled=True)
     inputs = lax.all_gather(got[:, :part], "expert", axis=1, tiled=True)
-    upward = lax.all_gather(got[:, part : 2 * part], "expert", axis=1, tiled=True)
+    upward = jnp.concatenate(lax.all_gather(got[:, part : 2 * part], "expert"), axis=1)
     scale_col = got[:, 2 * part : 2 * part + 1].astype(jnp.float32)
     piece, term, grad_gate, grad_up, grad_down = expert_backward(
         inputs, upward, scale_col, w_gate[0], w_up[0], w_down[0]

time: 250 us -> 254 us (1.016)
  local copies, waits for them, and re-layouts: 5.38 us -> 13.2 us
  matrix products: 37.9 us -> 32.6 us
    reshape x0 -> x1, local copies, waits for them, and re-layouts: none -> 6.2 us  [per_device(): jnp.concatenate(lax.all_gather(got[:, part:2 * part], 'expert'), axis=1)]
    dot_general x3, matrix products: 14.1 us -> 8.84 us  [contract_last(): lax.dot_general(left, right, (((1,), (1,)), ((), ())), preferred_element_...]
    all_gather x1, waiting for transfers between devices: 28.9 us -> 31.5 us  [per_device(): lax.all_gather(got[:, part:2 * part], 'expert')]
  transfers between devices with their start and end apart: 4 -> 4, of which waited for: 4 -> 4; matrix products, arithmetic and copies ran while one was open for 9% -> 8% of each run, Pallas kernels for 0% -> 0%
where the time goes in v1:
time: 254 us
  waiting for transfers between devices  117 us (46%)
  blocking collectives  64.4 us (25%)
  matrix products  32.6 us (13%)
  between operations  13.9 us (5%)
  local copies, waits for them, and re-layouts  13.2 us (5%)
  other arithmetic  7.49 us (3%)
  starting transfers between devices  5.63 us (2%)
    all_to_all x1, blocking collectives, per_device(): got = lax.all_to_all(send, 'dp', split_axis=0, concat_axis=0, tiled=True)  58.5 us
    reduce_scatter x1, waiting for transfers between devices, per_device(): summed = lax.psum_scatter(piece, 'expert', scatter_dimension=1, tiled=True)  38.4 us
    all_gather x1, waiting for transfers between devices, per_device(): lax.all_gather(got[:, part:2 * part], 'expert')  31.5 us
    all_gather x1, waiting for transfers between devices, per_device(): inputs = lax.all_gather(got[:, :part], 'expert', axis=1, tiled=True)  30.4 us
    all_to_all x1, waiting for transfers between devices, per_device(): lax.all_to_all(jnp.concatenate([summed, tail], axis=1), 'dp', split_axis=...  15.6 us
    dot_general x4, matrix products, contract_first(): lax.dot_general(left, right, (((0,), (0,)), ((), ())), preferred_element_...  15.1 us
    dot_general x3, matrix products, contract_last(): lax.dot_general(left, right, (((1,), (1,)), ((), ())), preferred_element_...  8.84 us
    reshape x1, local copies, waits for them, and re-layouts, per_device(): jnp.concatenate(lax.all_gather(got[:, part:2 * part], 'expert'), axis=1)  6.2 us
  transfers between devices with their start and end apart: 4, of which 4 were waited for; matrix products, arithmetic and copies ran while one was open for 8% of the time, Pallas kernels for 0%

profile of v1, /device:TPU:0, one launch (start us, length us, event | category | flops | bytes accessed | tf_op | source)
XLA Modules:
  0.0 253.8 jit_solution(10908962109142438467)
XLA Ops:
  7.2 0.9 copy.30
  8.7 0.7 multiply_add_fusion
  9.4 0.7 convert_element_type.79
  10.1 1.0 constant_dynamic-slice_fusion
  11.2 1.6 convolution_convert_fusion.3
  13.2 58.5 %all_to_all.24 = bf16[8,64,2176]{2,1,0:T(8,128)(2,1)S(1)} all-to-all(bf16[8,64,2176]{2,1,0:T(8,128)(2,1)S(1)} %bitcast.43), channel_id=1, replica_groups=mesh['dp'=8,'expert'=4] {'dp'}, dimensions={0} | all-to-all | bytes 4456448 | tf_op jit(solution)/shard_map/all_to_all | solution.py:68
  71.7 1.4 copy-done.1
  73.0 1.6 fusion.25
  74.7 0.7 all-gather.4.cloned.1.call-update
  75.5 1.0 convert_reduce_fusion.1
  76.5 31.5 %all-gather.6.cloned.1.call-done = bf16[2048,1024]{1,0:T(8,128)(2,1)} async-done(((bf16[512,1024]{1,0:T(8,128)(2,1)}), bf16[2048,1024]{1,0:T(8,128)(2,1)}) %all-gather.6.cloned.1.call-update) | async-done | bytes 4194320 | tf_op jit(solution)/shard_map/all_gather | solution.py:70
  108.0 6.2 %copy.32 = bf16[512,4,1024]{0,2,1:T(8,128)(2,1)} copy(bf16[512,4,1024]{2,0,1:T(8,128)(2,1)} %bitcast.47) | data formatting | bytes 8388608 | tf_op jit(solution)/shard_map/reshape | solution.py:70
  114.2 30.4 %all-gather.4.cloned.1.call-done = bf16[512,4096]{1,0:T(8,128)(2,1)} async-done(((bf16[512,1024]{1,0:T(8,128)(2,1)}), bf16[512,4096]{1,0:T(8,128)(2,1)}) %all-gather.4.cloned.1.call-update) | async-done | bytes 4194320 | tf_op jit(solution)/shard_map/all_gather | solution.py:69
  144.6 4.2 %fusion.5 = f32[512,384]{0,1:T(8,128)S(1)} fusion(bf16[512,4096]{1,0:T(8,128)(2,1)} %all-gather.4.cloned.1.call-done, bf16[1,384,4096]{2,1,0:T(8,128)(2,1)S(1)} %copy-done), kind=kOutput, calls=%fused_computation.9 | convolution fusion | flops 1610612736 | bytes 8126464 | tf_op jit(solution)/shard_map/dot_general | solution.py:13
  148.8 0.2 copy-done.8
  149.0 1.8 fusion.8
  150.8 0.4 copy-done.2
  151.2 1.0 copy-done.10
  152.2 2.9 %fusion.13 = (f32[512]{0:T(512)S(1)}, bf16[512,384]{0,1:T(8,128)(2,1)}, bf16[512,384]{0,1:T(8,128)(2,1)S(1)}, bf16[512,384]{0,1:T(8,128)(2,1)S(1)}) fusion(f32[512,384]{0,1:T(8,128)S(1)} %fusion.8, f32[512,384]{0,1:T(8,128)S(1)} %fusion.5, f32[512]{0:T(512)S(1)} %convert_reduce_fusion.1, bf16[512,4096]{0,1:T(8,128)(2,1)S(1)} %bitcast.45, ...), kind=kOutput, calls=%fused_computation.23 | convolution fusion | flops 1614347776 | bytes 10096640 | tf_op jit(solution)/shard_map/dot_general | solution.py:13
  155.0 2.4 fusion.3
  157.5 4.6 %add_convert_fusion = bf16[512,4096]{1,0:T(8,128)(2,1)} fusion(f32[512,4096]{1,0:T(8,128)S(1)} %fusion.3, bf16[512,384]{0,1:T(8,128)(2,1)S(1)} %get-tuple-element.14, bf16[1,384,4096]{2,1,0:T(8,128)(2,1)S(1)} %copy-done.4), kind=kOutput, calls=%fused_computation | convolution fusion | flops 1614807040 | bytes 16121856 | tf_op jit(solution)/shard_map/dot_general | solution.py:40
  162.1 5.9 %psum.7 = f32[512]{0:T(512)S(1)} all-reduce(f32[512]{0:T(512)S(1)} %get-tuple-element.9), channel_id=1, replica_groups=mesh['dp'=8,'expert'=4] {'expert'}, use_global_device_ids=true, to_apply=%region_5.6 | all-reduce | flops 512 | bytes 4096 | tf_op jit(solution)/shard_map/psum | solution.py:75
  168.2 38.4 %reduce-scatter.2.cloned.1.call-done = bf16[512,1024]{1,0:T(8,128)(2,1)} async-done(((bf16[512,4096]{1,0:T(8,128)(2,1)}), bf16[512,1024]{1,0:T(8,128)(2,1)}) %reduce-scatter.2.cloned.1.call-update) | async-done | bytes 1048592 | tf_op jit(solution)/shard_map/reduce_scatter | solution.py:76
  206.6 2.4 pad_maximum_fusion.1
  209.1 5.5 %all-to-all-start.1 = ((bf16[8,64,1152]{2,1,0:T(8,128)(2,1)}), bf16[8,64,1152]{2,1,0:T(8,128)(2,1)}, u32[]{:S(2)}, u32[]{:S(2)}) async-start(bf16[8,64,1152]{2,1,0:T(8,128)(2,1)} %bitcast.44), calls=%async_computation.2 | async-start | bytes 2359296 | tf_op jit(solution)/shard_map/all_to_all | solution.py:81
  214.6 5.9 %fusion = bf16[1,384,4096]{2,1,0:T(8,128)(2,1)} fusion(bf16[512,384]{0,1:T(8,128)(2,1)} %copy-done.7, bf16[512,4096]{1,0:T(8,128)(2,1)} %all-gather.4.cloned.1.call-done), kind=kOutput, calls=%fused_computation.4 | convolution fusion | flops 1612185600 | bytes 7733248 | tf_op jit(solution)/shard_map/dot_general | solution.py:19
  220.5 3.5 %fusion.1 = bf16[1,384,4096]{2,1,0:T(8,128)(2,1)} fusion(bf16[512,384]{0,1:T(8,128)(2,1)S(1)} %copy-done.6, bf16[512,4096]{1,0:T(8,128)(2,1)S(1)} %copy-done.9), kind=kOutput, calls=%fused_computation.5 | convolution fusion | flops 1612185600 | bytes 7733248 | tf_op jit(solution)/shard_map/dot_general | solution.py:19
  224.0 3.5 %fusion.2 = bf16[1,384,4096]{2,1,0:T(8,128)(2,1)} fusion(bf16[512,4096]{0,1:T(8,128)(2,1)S(1)} %bitcast.46, bf16[512,384]{0,1:T(8,128)(2,1)S(1)} %copy-done.11, f32[512]{0:T(512)S(1)} %convert_reduce_fusion.1), kind=kOutput, calls=%fused_computation.6 | convolution fusion | flops 1612775424 | bytes 7735296 | tf_op jit(solution)/shard_map/dot_general | solution.py:19
  227.5 15.6 %all-to-all-done.1 = bf16[8,64,1152]{2,1,0:T(8,128)(2,1)} async-done(((bf16[8,64,1152]{2,1,0:T(8,128)(2,1)}), bf16[8,64,1152]{2,1,0:T(8,128)(2,1)}, u32[]{:S(2)}, u32[]{:S(2)}) %all-to-all-start.1) | async-done | bytes 1179680 | tf_op jit(solution)/shard_map/all_to_all | solution.py:81
  243.1 2.3 convolution_convert_fusion.4
  245.4 1.2 add_reduce_fusion
  246.6 0.7 select_reduce_fusion
  (35 shorter events, 1.4 us)
Async XLA Ops:
  7.2 137.4 %copy-start = (bf16[1,384,4096]{2,1,0:T(8,128)(2,1)S(1)}, bf16[1,384,4096]{2,1,0:T(8,128)(2,1)}, u32[]{:S(2)}) copy-start(bf16[1,384,4096]{2,1,0:T(8,128)(2,1)} %param.11) | copy-start | bytes 9437188
  7.2 100.8 %all-gather.6.cloned.1.call-start = ((), (), s32[]{:S(2)}) async-start(), calls=%async_computation.5 | async-start | bytes 5242880 | tf_op jit(solution)/shard_map/all_gather | solution.py:70
  71.7 1.4 copy-start.1
  74.7 69.9 %all-gather.4.cloned.1.call-start = ((), (), s32[]{:S(2)}) async-start(), calls=%async_computation.3 | async-start | bytes 5242880 | tf_op jit(solution)/shard_map/all_gather | solution.py:69
  75.4 131.2 %reduce-scatter.2.cloned.1.call-start = ((), (), s32[]{:S(2)}) async-start(), calls=%async_computation.4 | async-start | bytes 5242880 | tf_op jit(solution)/shard_map/reduce_scatter | solution.py:76
  144.6 4.2 %copy-start.4 = (bf16[1,384,4096]{2,1,0:T(8,128)(2,1)S(1)}, bf16[1,384,4096]{2,1,0:T(8,128)(2,1)}, u32[]{:S(2)}) copy-start(bf16[1,384,4096]{2,1,0:T(8,128)(2,1)} %param.12) | copy-start | bytes 9437188
  144.6 4.4 %copy-start.8 = (bf16[512,4096]{1,0:T(8,128)(2,1)S(1)}, bf16[512,4096]{1,0:T(8,128)(2,1)}, u32[]{:S(2)}) copy-start(bf16[512,4096]{1,0:T(8,128)(2,1)} %all-gather.4.cloned.1.call-done) | copy-start | bytes 12582916
  149.0 2.2 copy-start.2
  149.0 3.2 %copy-start.10 = (bf16[1,384,4096]{2,1,0:T(8,128)(2,1)S(1)}, bf16[1,384,4096]{2,1,0:T(8,128)(2,1)}, u32[]{:S(2)}) copy-start(bf16[1,384,4096]{2,1,0:T(8,128)(2,1)} %param.13) | copy-start | bytes 9437188
  155.0 2.4 copy-start.7
  155.0 2.4 copy-start.5
  209.1 34.0 %all-to-all-start.1 = ((bf16[8,64,1152]{2,1,0:T(8,128)(2,1)}), bf16[8,64,1152]{2,1,0:T(8,128)(2,1)}, u32[]{:S(2)}, u32[]{:S(2)}) async-start(bf16[8,64,1152]{2,1,0:T(8,128)(2,1)} %bitcast.44), calls=%async_computation.2 | async-start | bytes 2359296 | tf_op jit(solution)/shard_map/all_to_all | solution.py:81
  214.6 5.9 %copy-start.6 = (bf16[512,384]{0,1:T(8,128)(2,1)S(1)}, bf16[512,384]{0,1:T(8,128)(2,1)}, u32[]{:S(2)}) copy-start(bf16[512,384]{0,1:T(8,128)(2,1)} %copy-done.5) | copy-start | bytes 1179652
  214.6 5.9 %copy-start.9 = (bf16[512,4096]{1,0:T(8,128)(2,1)S(1)}, bf16[512,4096]{1,0:T(8,128)(2,1)}, u32[]{:S(2)}) copy-start(bf16[512,4096]{1,0:T(8,128)(2,1)} %all-gather.4.cloned.1.call-done) | copy-start | bytes 12582916
  220.5 3.5 %copy-start.3 = (bf16[512,4,1024]{0,2,1:T(8,128)(2,1)S(1)}, bf16[512,4,1024]{0,2,1:T(8,128)(2,1)}, u32[]{:S(2)}) copy-start(bf16[512,4,1024]{0,2,1:T(8,128)(2,1)} %copy.32) | copy-start | bytes 12582916
  220.5 3.5 %copy-start.11 = (bf16[512,384]{0,1:T(8,128)(2,1)S(1)}, bf16[512,384]{0,1:T(8,128)(2,1)}, u32[]{:S(2)}) copy-start(bf16[512,384]{0,1:T(8,128)(2,1)} %get-tuple-element.10) | copy-start | bytes 1179652
Sparse Core Ops, SparseCore 0:
  74.8 33.1 all-gather.5
  110.1 34.4 all-gather.3
  162.2 44.3 reduce-scatter.1
